TPU v7x, 32 devices: a whole 2x2x4 slice. The times are simulated.
32 devices in a mesh: tm: 8 (over z, x), lon: 4 (over y, core).
Axes of the slice: x: 2, y: 2, z: 4, core: 2. Of those that a mesh axis runs over, the one named last changes fastest.
Arguments:
- start: float32 [3, 128, 512], P(None, 'lon'), may hold values from -6 to 6
- depth: float32 [128, 512], P('lon'), may hold values from 0.5 to 1.5
Outputs:
- ends: float32 [8, 3, 128, 512], P('tm', None, 'lon')
All inputs are finite; a program needn't handle non-finite values.
Results may differ from a plain program's by a relative error of at most 0.00002.
Values sent between devices are 32-bit elements; how exact they have to be, the bound alone decides.
No kernel may reach another device: no remote copies, remote signals or barrier semaphores. Data moves between devices by JAX's collectives and lax.ppermute only.
A program may use at most 64 MiB of HBM per device.

v0:
```python
import math
import jax
import jax.numpy as jnp
from jax import lax
from jax.sharding import PartitionSpec as P

STEPS = 3
ROUNDS = 2
LAT_LIMIT = 1.2
COURANT = 1.2
DEPTH_MAX = 1.5
GRAVITY = 1.0
TURN_RATE = 0.15


def padded_2(cells, sides, width):
    for axis, dim in sides:
        count = lax.axis_size(axis)
        head = lax.slice_in_dim(cells, 0, width, axis=dim)
        tail = lax.slice_in_dim(cells, cells.shape[dim] - width, cells.shape[dim], axis=dim)
        cells = jnp.concatenate(
            [
                lax.ppermute(tail, axis, [(i, (i + 1) % count) for i in range(count)]),
                cells,
                lax.ppermute(head, axis, [((i + 1) % count, i) for i in range(count)]),
            ],
            axis=dim,
        )
    return cells


def grid_constants(lon_cells, lat_cells):
    latitude = -LAT_LIMIT + (jnp.arange(lat_cells, dtype=jnp.float32) + 0.5) * (
        2.0 * LAT_LIMIT / lat_cells
    )
    cosine = jnp.cos(latitude)
    north_spacing = 2.0 * LAT_LIMIT / lat_cells
    east_spacing = cosine * (2.0 * math.pi / lon_cells)
    narrowest = math.cos(LAT_LIMIT - LAT_LIMIT / lat_cells) * 2.0 * math.pi / lon_cells
    time_step = COURANT / (
        math.sqrt(DEPTH_MAX * GRAVITY) * math.sqrt(1.0 / narrowest**2 + 1.0 / north_spacing**2)
    )
    coriolis = TURN_RATE * jnp.sin(latitude) / time_step
    turning = coriolis * (STEPS * time_step)
    return (cosine, east_spacing, north_spacing, time_step, coriolis, turning)


def north_diff(values):
    padded = jnp.pad(values, ((0, 0), (1, 1)))
    return padded[:, 2:] - padded[:, :-2]


def advance_split(state, depth, consts):
    cosine, east_spacing, north_spacing, time_step, coriolis, turning = consts
    height = state[0]
    zonal = state[1]
    merid = state[2]
    flux_wide = padded_2(depth * zonal, (("lon", 0),), 1)
    flux_north = depth * merid * cosine
    diverge = (flux_wide[2:] - flux_wide[:-2]) / (2.0 * east_spacing) + north_diff(flux_north) / (
        2.0 * north_spacing * cosine
    )
    height_new = height - time_step * diverge
    height_wide = padded_2(height_new, (("lon", 0),), 1)
    zonal_new = zonal + time_step * (
        coriolis * merid - GRAVITY * (height_wide[2:] - height_wide[:-2]) / (2.0 * east_spacing)
    )
    merid_new = merid + time_step * (
        -coriolis * zonal_new - GRAVITY * north_diff(height_new) / (2.0 * north_spacing)
    )
    return jnp.stack([height_new, zonal_new, merid_new])


def rotate(state, angle):
    cos_angle = jnp.cos(angle)
    sin_angle = jnp.sin(angle)
    zonal = state[..., 1, :, :]
    merid = state[..., 2, :, :]
    return jnp.stack(
        [
            state[..., 0, :, :],
            zonal * cos_angle + merid * sin_angle,
            merid * cos_angle - zonal * sin_angle,
        ],
        axis=-3,
    )


def body(start, depth):
    lon_cells = start.shape[1] * lax.axis_size("lon")
    lat_cells = start.shape[2]
    consts = grid_constants(lon_cells, lat_cells)
    turning = consts[5]
    number = lax.axis_index("tm").astype(jnp.float32)
    guess = rotate(start, number * turning)
    ends = guess
    for round_index in range(ROUNDS):
        state = guess
        for turn_index in range(STEPS):
            state = advance_split(state, depth, consts)
        correct = state - rotate(guess, turning)
        carried = rotate(correct, -(number + 1.0) * turning)
        stacked = lax.all_to_all(carried[None], "tm", split_axis=2, concat_axis=0, tiled=True)
        running = jnp.cumsum(stacked, axis=0)
        running = jnp.concatenate([jnp.zeros_like(stacked[:1]), running[:-1]], axis=0)
        before = lax.all_to_all(running, "tm", split_axis=0, concat_axis=2, tiled=True)[0]
        total = start + before
        if round_index + 1 < ROUNDS:
            guess = rotate(total, number * turning)
        else:
            ends = rotate(total + carried, (number + 1.0) * turning)
    return ends[None]


def solution(mesh):
    return jax.shard_map(
        body,
        mesh=mesh,
        in_specs=(P(None, "lon", None), P("lon", None)),
        out_specs=P("tm", None, "lon", None),
        check_vma=False,
    )
```

profile of v0, /device:TPU:0, one launch (start us, length us, event | category | flops | bytes accessed | tf_op | source)
XLA Modules:
  0.0 90.6 jit_solution(3166907388512287676)
XLA Ops:
  0.1 0.1 fusion.124
  0.2 1.0 %multiply_multiply_fusion.5 = (f32[32,512]{1,0:T(8,128)S(1)}, f32[32,512]{1,0:T(8,128)S(1)}, f32[32,512]{1,0:T(8,128)S(1)}) fusion(f32[32,512]{1,0:T(8,128)} %param.3, f32[512]{0:T(512)S(1)} %fusion.117, f32[512]{0:T(512)S(1)} %get-tuple-element.70, f32[3,32,512]{2,1,0:T(8,128)} %param.2, f32[512]{0:T(512)S(1)} %get-tuple-element.71), kind=kLoop, calls=%fused_computation.196 | loop fusion | flops 147456 | bytes 399360 | tf_op jit(solution)/shard_map/mul | solution.py:59
  1.1 2.5 %collective-permute-start = (f32[1,512]{1,0:T(1,128)S(1)}, f32[1,512]{1,0:T(1,128)S(1)}, u32[]{:S(2)}, u32[]{:S(2)}) collective-permute-start(f32[1,512]{1,0:T(1,128)S(1)} %get-tuple-element.68), channel_id=1, source_target_pairs={{1,0},{2,1},{3,2},{0,3},{5,4},{6,5},{7,6},{4,7},{9,8},{10,9},{11,1... | collective-permute-start | bytes 6152 | tf_op jit(solution)/shard_map/ppermute | solution.py:25
  3.7 0.1 fusion.126
  3.8 1.1 %collective-permute-done = f32[1,512]{1,0:T(1,128)S(1)} collective-permute-done((f32[1,512]{1,0:T(1,128)S(1)}, f32[1,512]{1,0:T(1,128)S(1)}, u32[]{:S(2)}, u32[]{:S(2)}) %collective-permute-start) | collective-permute-done | bytes 2080 | tf_op jit(solution)/shard_map/ppermute | solution.py:25
  4.9 1.7 %collective-permute-done.1 = f32[1,512]{1,0:T(1,128)S(1)} collective-permute-done((f32[1,512]{1,0:T(1,128)S(1)}, f32[1,512]{1,0:T(1,128)S(1)}, u32[]{:S(2)}, u32[]{:S(2)}) %collective-permute-start.1) | collective-permute-done | bytes 2080 | tf_op jit(solution)/shard_map/ppermute | solution.py:23
  6.6 0.1 fusion.11
  6.8 0.5 collective-permute-start.3
  7.4 0.8 collective-permute-done.2
  8.1 1.8 %collective-permute-done.3 = f32[1,512]{1,0:T(1,128)S(1)} collective-permute-done((f32[1,512]{1,0:T(1,128)S(1)}, f32[1,512]{1,0:T(1,128)S(1)}, u32[]{:S(2)}, u32[]{:S(2)}) %collective-permute-start.3) | collective-permute-done | bytes 2080 | tf_op jit(solution)/shard_map/ppermute | solution.py:23
  10.0 0.5 collective-permute-start.5
  10.5 0.1 multiply_multiply_fusion.4
  10.6 0.7 collective-permute-done.4
  11.3 1.8 %collective-permute-done.5 = f32[1,512]{1,0:T(1,128)S(1)} collective-permute-done((f32[1,512]{1,0:T(1,128)S(1)}, f32[1,512]{1,0:T(1,128)S(1)}, u32[]{:S(2)}, u32[]{:S(2)}) %collective-permute-start.5) | collective-permute-done | bytes 2080 | tf_op jit(solution)/shard_map/ppermute | solution.py:23
  13.1 0.1 fusion.21
  13.3 0.5 collective-permute-start.7
  13.8 0.8 collective-permute-done.6
  14.6 1.8 %collective-permute-done.7 = f32[1,512]{1,0:T(1,128)S(1)} collective-permute-done((f32[1,512]{1,0:T(1,128)S(1)}, f32[1,512]{1,0:T(1,128)S(1)}, u32[]{:S(2)}, u32[]{:S(2)}) %collective-permute-start.7) | collective-permute-done | bytes 2080 | tf_op jit(solution)/shard_map/ppermute | solution.py:23
  16.5 0.5 collective-permute-start.9
  17.0 0.1 multiply_multiply_fusion.3
  17.1 0.7 collective-permute-done.8
  17.8 1.8 %collective-permute-done.9 = f32[1,512]{1,0:T(1,128)S(1)} collective-permute-done((f32[1,512]{1,0:T(1,128)S(1)}, f32[1,512]{1,0:T(1,128)S(1)}, u32[]{:S(2)}, u32[]{:S(2)}) %collective-permute-start.9) | collective-permute-done | bytes 2080 | tf_op jit(solution)/shard_map/ppermute | solution.py:23
  19.5 0.1 fusion.31
  19.7 0.5 collective-permute-start.11
  20.2 0.1 fusion.128
  20.3 0.7 collective-permute-done.10
  21.0 1.8 %collective-permute-done.11 = f32[1,512]{1,0:T(1,128)S(1)} collective-permute-done((f32[1,512]{1,0:T(1,128)S(1)}, f32[1,512]{1,0:T(1,128)S(1)}, u32[]{:S(2)}, u32[]{:S(2)}) %collective-permute-start.11) | collective-permute-done | bytes 2080 | tf_op jit(solution)/shard_map/ppermute | solution.py:23
  22.8 0.1 fusion.133
  23.0 0.2 copy.63
  23.2 13.4 %all_to_all.66 = f32[1,3,32,512]{3,0,1,2:T(1,128)S(1)} all-to-all(f32[1,3,32,512]{3,0,1,2:T(1,128)S(1)} %copy.63), channel_id=1, replica_groups=mesh['tm'=8,'lon'=4] {'tm'}, dimensions={2} | all-to-all | bytes 393216 | tf_op jit(solution)/shard_map/all_to_all | solution.py:103
  36.8 10.2 %all_to_all.67 = f32[8,3,4,512]{3,2,1,0:T(4,128)S(1)} all-to-all(f32[8,3,4,512]{3,2,1,0:T(4,128)S(1)} %concatenate.102.clone), channel_id=1, replica_groups=mesh['tm'=8,'lon'=4] {'tm'}, dimensions={0} | all-to-all | bytes 393216 | tf_op jit(solution)/shard_map/all_to_all | solution.py:106
  47.0 0.1 squeeze.26
  47.2 0.5 collective-permute-start.13
  47.7 0.8 collective-permute-done.12
  48.5 1.8 %collective-permute-done.13 = f32[1,512]{1,0:T(1,128)S(1)} collective-permute-done((f32[1,512]{1,0:T(1,128)S(1)}, f32[1,512]{1,0:T(1,128)S(1)}, u32[]{:S(2)}, u32[]{:S(2)}) %collective-permute-start.13) | collective-permute-done | bytes 2080 | tf_op jit(solution)/shard_map/ppermute | solution.py:23
  50.3 0.1 fusion.42
  50.5 0.5 collective-permute-start.15
  51.0 0.8 collective-permute-done.14
  51.8 1.8 %collective-permute-done.15 = f32[1,512]{1,0:T(1,128)S(1)} collective-permute-done((f32[1,512]{1,0:T(1,128)S(1)}, f32[1,512]{1,0:T(1,128)S(1)}, u32[]{:S(2)}, u32[]{:S(2)}) %collective-permute-start.15) | collective-permute-done | bytes 2080 | tf_op jit(solution)/shard_map/ppermute | solution.py:23
  53.7 0.5 collective-permute-start.17
  54.2 0.1 multiply_multiply_fusion.1
  54.3 0.7 collective-permute-done.16
  55.0 1.8 %collective-permute-done.17 = f32[1,512]{1,0:T(1,128)S(1)} collective-permute-done((f32[1,512]{1,0:T(1,128)S(1)}, f32[1,512]{1,0:T(1,128)S(1)}, u32[]{:S(2)}, u32[]{:S(2)}) %collective-permute-start.17) | collective-permute-done | bytes 2080 | tf_op jit(solution)/shard_map/ppermute | solution.py:23
  56.7 0.1 fusion.52
  56.9 0.5 collective-permute-start.19
  57.4 0.8 collective-permute-done.18
  58.2 1.8 %collective-permute-done.19 = f32[1,512]{1,0:T(1,128)S(1)} collective-permute-done((f32[1,512]{1,0:T(1,128)S(1)}, f32[1,512]{1,0:T(1,128)S(1)}, u32[]{:S(2)}, u32[]{:S(2)}) %collective-permute-start.19) | collective-permute-done | bytes 2080 | tf_op jit(solution)/shard_map/ppermute | solution.py:23
  60.1 0.5 collective-permute-start.21
  60.6 0.1 multiply_multiply_fusion
  60.7 0.7 collective-permute-done.20
  61.4 1.8 %collective-permute-done.21 = f32[1,512]{1,0:T(1,128)S(1)} collective-permute-done((f32[1,512]{1,0:T(1,128)S(1)}, f32[1,512]{1,0:T(1,128)S(1)}, u32[]{:S(2)}, u32[]{:S(2)}) %collective-permute-start.21) | collective-permute-done | bytes 2080 | tf_op jit(solution)/shard_map/ppermute | solution.py:23
  63.2 0.1 fusion.62
  63.4 0.5 collective-permute-start.23
  63.9 0.8 collective-permute-done.22
  64.7 1.8 %collective-permute-done.23 = f32[1,512]{1,0:T(1,128)S(1)} collective-permute-done((f32[1,512]{1,0:T(1,128)S(1)}, f32[1,512]{1,0:T(1,128)S(1)}, u32[]{:S(2)}, u32[]{:S(2)}) %collective-permute-start.23) | collective-permute-done | bytes 2080 | tf_op jit(solution)/shard_map/ppermute | solution.py:23
  66.4 0.1 fusion.134
  66.6 0.2 copy.67
  66.8 10.9 %all_to_all.68 = f32[1,3,32,512]{3,0,1,2:T(1,128)S(1)} all-to-all(f32[1,3,32,512]{3,0,1,2:T(1,128)S(1)} %copy.67), channel_id=1, replica_groups=mesh['tm'=8,'lon'=4] {'tm'}, dimensions={2} | all-to-all | bytes 393216 | tf_op jit(solution)/shard_map/all_to_all | solution.py:103
  77.9 0.7 concatenate.115.clone
  78.6 3.4 %all-to-all-start.3 = ((f32[8,3,4,512]{3,2,1,0:T(4,128)}), f32[8,3,4,512]{3,2,1,0:T(4,128)S(1)}, u32[]{:S(2)}, u32[]{:S(2)}) async-start(f32[8,3,4,512]{3,2,1,0:T(4,128)} %concatenate.115.clone), calls=%async_computation.3 | async-start | bytes 393216 | tf_op jit(solution)/shard_map/all_to_all | solution.py:106
  82.0 0.1 fusion.130
  82.1 7.6 %all-to-all-done.3 = f32[8,3,4,512]{3,2,1,0:T(4,128)S(1)} async-done(((f32[8,3,4,512]{3,2,1,0:T(4,128)}), f32[8,3,4,512]{3,2,1,0:T(4,128)S(1)}, u32[]{:S(2)}, u32[]{:S(2)}) %all-to-all-start.3) | async-done | bytes 196640 | tf_op jit(solution)/shard_map/all_to_all | solution.py:106
  89.7 0.1 squeeze.29
  89.9 0.7 maximum_bitcast_fusion.1
  (59 shorter events, 1.7 us)
Async XLA Ops:
  0.1 6.5 %copy-start.1 = (f32[3,32,512]{2,1,0:T(8,128)S(1)}, f32[3,32,512]{2,1,0:T(8,128)}, u32[]{:S(2)}) copy-start(f32[3,32,512]{2,1,0:T(8,128)} %param.2) | copy-start | bytes 589828
  1.1 3.8 %collective-permute-start = (f32[1,512]{1,0:T(1,128)S(1)}, f32[1,512]{1,0:T(1,128)S(1)}, u32[]{:S(2)}, u32[]{:S(2)}) collective-permute-start(f32[1,512]{1,0:T(1,128)S(1)} %get-tuple-element.68), channel_id=1, source_target_pairs={{1,0},{2,1},{3,2},{0,3},{5,4},{6,5},{7,6},{4,7},{9,8},{10,9},{11,1... | collective-permute-start | bytes 6152 | tf_op jit(solution)/shard_map/ppermute | solution.py:25
  3.6 3.0 %collective-permute-start.1 = (f32[1,512]{1,0:T(1,128)S(1)}, f32[1,512]{1,0:T(1,128)S(1)}, u32[]{:S(2)}, u32[]{:S(2)}) collective-permute-start(f32[1,512]{1,0:T(1,128)S(1)} %get-tuple-element.69), channel_id=1, source_target_pairs={{0,1},{1,2},{2,3},{3,0},{4,5},{5,6},{6,7},{7,4},{8,9},{9,10},{10,1... | collective-permute-start | bytes 6152 | tf_op jit(solution)/shard_map/ppermute | solution.py:23
  6.6 3.3 %copy-start = (f32[32,512]{1,0:T(8,128)S(1)}, f32[32,512]{1,0:T(8,128)}, u32[]{:S(2)}) copy-start(f32[32,512]{1,0:T(8,128)} %param.3) | copy-start | bytes 196612
  6.8 1.4 %collective-permute-start.2 = (f32[1,512]{1,0:T(1,128)S(1)}, f32[1,512]{1,0:T(1,128)S(1)}, u32[]{:S(2)}, u32[]{:S(2)}) collective-permute-start(f32[1,512]{1,0:T(1,128)S(1)} %get-tuple-element.66), channel_id=1, source_target_pairs={{1,0},{2,1},{3,2},{0,3},{5,4},{6,5},{7,6},{4,7},{9,8},{10,9},{11,1... | collective-permute-start | bytes 6152 | tf_op jit(solution)/shard_map/ppermute | solution.py:25
  6.8 3.1 %collective-permute-start.3 = (f32[1,512]{1,0:T(1,128)S(1)}, f32[1,512]{1,0:T(1,128)S(1)}, u32[]{:S(2)}, u32[]{:S(2)}) collective-permute-start(f32[1,512]{1,0:T(1,128)S(1)} %get-tuple-element.67), channel_id=1, source_target_pairs={{0,1},{1,2},{2,3},{3,0},{4,5},{5,6},{6,7},{7,4},{8,9},{9,10},{10,1... | collective-permute-start | bytes 6152 | tf_op jit(solution)/shard_map/ppermute | solution.py:23
  10.0 1.4 %collective-permute-start.4 = (f32[1,512]{1,0:T(1,128)S(1)}, f32[1,512]{1,0:T(1,128)S(1)}, u32[]{:S(2)}, u32[]{:S(2)}) collective-permute-start(f32[1,512]{1,0:T(1,128)S(1)} %get-tuple-element.64), channel_id=1, source_target_pairs={{1,0},{2,1},{3,2},{0,3},{5,4},{6,5},{7,6},{4,7},{9,8},{10,9},{11,1... | collective-permute-start | bytes 6152 | tf_op jit(solution)/shard_map/ppermute | solution.py:25
  10.0 3.1 %collective-permute-start.5 = (f32[1,512]{1,0:T(1,128)S(1)}, f32[1,512]{1,0:T(1,128)S(1)}, u32[]{:S(2)}, u32[]{:S(2)}) collective-permute-start(f32[1,512]{1,0:T(1,128)S(1)} %get-tuple-element.65), channel_id=1, source_target_pairs={{0,1},{1,2},{2,3},{3,0},{4,5},{5,6},{6,7},{7,4},{8,9},{9,10},{10,1... | collective-permute-start | bytes 6152 | tf_op jit(solution)/shard_map/ppermute | solution.py:23
  13.2 1.4 %collective-permute-start.6 = (f32[1,512]{1,0:T(1,128)S(1)}, f32[1,512]{1,0:T(1,128)S(1)}, u32[]{:S(2)}, u32[]{:S(2)}) collective-permute-start(f32[1,512]{1,0:T(1,128)S(1)} %get-tuple-element.62), channel_id=1, source_target_pairs={{1,0},{2,1},{3,2},{0,3},{5,4},{6,5},{7,6},{4,7},{9,8},{10,9},{11,1... | collective-permute-start | bytes 6152 | tf_op jit(solution)/shard_map/ppermute | solution.py:25
  13.3 3.1 %collective-permute-start.7 = (f32[1,512]{1,0:T(1,128)S(1)}, f32[1,512]{1,0:T(1,128)S(1)}, u32[]{:S(2)}, u32[]{:S(2)}) collective-permute-start(f32[1,512]{1,0:T(1,128)S(1)} %get-tuple-element.63), channel_id=1, source_target_pairs={{0,1},{1,2},{2,3},{3,0},{4,5},{5,6},{6,7},{7,4},{8,9},{9,10},{10,1... | collective-permute-start | bytes 6152 | tf_op jit(solution)/shard_map/ppermute | solution.py:23
  16.4 1.4 %collective-permute-start.8 = (f32[1,512]{1,0:T(1,128)S(1)}, f32[1,512]{1,0:T(1,128)S(1)}, u32[]{:S(2)}, u32[]{:S(2)}) collective-permute-start(f32[1,512]{1,0:T(1,128)S(1)} %get-tuple-element.60), channel_id=1, source_target_pairs={{1,0},{2,1},{3,2},{0,3},{5,4},{6,5},{7,6},{4,7},{9,8},{10,9},{11,1... | collective-permute-start | bytes 6152 | tf_op jit(solution)/shard_map/ppermute | solution.py:25
  16.5 3.1 %collective-permute-start.9 = (f32[1,512]{1,0:T(1,128)S(1)}, f32[1,512]{1,0:T(1,128)S(1)}, u32[]{:S(2)}, u32[]{:S(2)}) collective-permute-start(f32[1,512]{1,0:T(1,128)S(1)} %get-tuple-element.61), channel_id=1, source_target_pairs={{0,1},{1,2},{2,3},{3,0},{4,5},{5,6},{6,7},{7,4},{8,9},{9,10},{10,1... | collective-permute-start | bytes 6152 | tf_op jit(solution)/shard_map/ppermute | solution.py:23
  19.7 1.4 %collective-permute-start.10 = (f32[1,512]{1,0:T(1,128)S(1)}, f32[1,512]{1,0:T(1,128)S(1)}, u32[]{:S(2)}, u32[]{:S(2)}) collective-permute-start(f32[1,512]{1,0:T(1,128)S(1)} %get-tuple-element.58), channel_id=1, source_target_pairs={{1,0},{2,1},{3,2},{0,3},{5,4},{6,5},{7,6},{4,7},{9,8},{10,9},{11,1... | collective-permute-start | bytes 6152 | tf_op jit(solution)/shard_map/ppermute | solution.py:25
  19.7 3.1 %collective-permute-start.11 = (f32[1,512]{1,0:T(1,128)S(1)}, f32[1,512]{1,0:T(1,128)S(1)}, u32[]{:S(2)}, u32[]{:S(2)}) collective-permute-start(f32[1,512]{1,0:T(1,128)S(1)} %get-tuple-element.59), channel_id=1, source_target_pairs={{0,1},{1,2},{2,3},{3,0},{4,5},{5,6},{6,7},{7,4},{8,9},{9,10},{10,1... | collective-permute-start | bytes 6152 | tf_op jit(solution)/shard_map/ppermute | solution.py:23
  47.2 1.4 %collective-permute-start.12 = (f32[1,512]{1,0:T(1,128)S(1)}, f32[1,512]{1,0:T(1,128)S(1)}, u32[]{:S(2)}, u32[]{:S(2)}) collective-permute-start(f32[1,512]{1,0:T(1,128)S(1)} %get-tuple-element.56), channel_id=1, source_target_pairs={{1,0},{2,1},{3,2},{0,3},{5,4},{6,5},{7,6},{4,7},{9,8},{10,9},{11,1... | collective-permute-start | bytes 6152 | tf_op jit(solution)/shard_map/ppermute | solution.py:25
  47.2 3.1 %collective-permute-start.13 = (f32[1,512]{1,0:T(1,128)S(1)}, f32[1,512]{1,0:T(1,128)S(1)}, u32[]{:S(2)}, u32[]{:S(2)}) collective-permute-start(f32[1,512]{1,0:T(1,128)S(1)} %get-tuple-element.57), channel_id=1, source_target_pairs={{0,1},{1,2},{2,3},{3,0},{4,5},{5,6},{6,7},{7,4},{8,9},{9,10},{10,1... | collective-permute-start | bytes 6152 | tf_op jit(solution)/shard_map/ppermute | solution.py:23
  50.4 1.4 %collective-permute-start.14 = (f32[1,512]{1,0:T(1,128)S(1)}, f32[1,512]{1,0:T(1,128)S(1)}, u32[]{:S(2)}, u32[]{:S(2)}) collective-permute-start(f32[1,512]{1,0:T(1,128)S(1)} %get-tuple-element.54), channel_id=1, source_target_pairs={{1,0},{2,1},{3,2},{0,3},{5,4},{6,5},{7,6},{4,7},{9,8},{10,9},{11,1... | collective-permute-start | bytes 6152 | tf_op jit(solution)/shard_map/ppermute | solution.py:25
  50.5 3.1 %collective-permute-start.15 = (f32[1,512]{1,0:T(1,128)S(1)}, f32[1,512]{1,0:T(1,128)S(1)}, u32[]{:S(2)}, u32[]{:S(2)}) collective-permute-start(f32[1,512]{1,0:T(1,128)S(1)} %get-tuple-element.55), channel_id=1, source_target_pairs={{0,1},{1,2},{2,3},{3,0},{4,5},{5,6},{6,7},{7,4},{8,9},{9,10},{10,1... | collective-permute-start | bytes 6152 | tf_op jit(solution)/shard_map/ppermute | solution.py:23
  53.6 1.4 %collective-permute-start.16 = (f32[1,512]{1,0:T(1,128)S(1)}, f32[1,512]{1,0:T(1,128)S(1)}, u32[]{:S(2)}, u32[]{:S(2)}) collective-permute-start(f32[1,512]{1,0:T(1,128)S(1)} %get-tuple-element.52), channel_id=1, source_target_pairs={{1,0},{2,1},{3,2},{0,3},{5,4},{6,5},{7,6},{4,7},{9,8},{10,9},{11,1... | collective-permute-start | bytes 6152 | tf_op jit(solution)/shard_map/ppermute | solution.py:25
  53.7 3.1 %collective-permute-start.17 = (f32[1,512]{1,0:T(1,128)S(1)}, f32[1,512]{1,0:T(1,128)S(1)}, u32[]{:S(2)}, u32[]{:S(2)}) collective-permute-start(f32[1,512]{1,0:T(1,128)S(1)} %get-tuple-element.53), channel_id=1, source_target_pairs={{0,1},{1,2},{2,3},{3,0},{4,5},{5,6},{6,7},{7,4},{8,9},{9,10},{10,1... | collective-permute-start | bytes 6152 | tf_op jit(solution)/shard_map/ppermute | solution.py:23
  56.9 1.4 %collective-permute-start.18 = (f32[1,512]{1,0:T(1,128)S(1)}, f32[1,512]{1,0:T(1,128)S(1)}, u32[]{:S(2)}, u32[]{:S(2)}) collective-permute-start(f32[1,512]{1,0:T(1,128)S(1)} %get-tuple-element.50), channel_id=1, source_target_pairs={{1,0},{2,1},{3,2},{0,3},{5,4},{6,5},{7,6},{4,7},{9,8},{10,9},{11,1... | collective-permute-start | bytes 6152 | tf_op jit(solution)/shard_map/ppermute | solution.py:25
  56.9 3.1 %collective-permute-start.19 = (f32[1,512]{1,0:T(1,128)S(1)}, f32[1,512]{1,0:T(1,128)S(1)}, u32[]{:S(2)}, u32[]{:S(2)}) collective-permute-start(f32[1,512]{1,0:T(1,128)S(1)} %get-tuple-element.51), channel_id=1, source_target_pairs={{0,1},{1,2},{2,3},{3,0},{4,5},{5,6},{6,7},{7,4},{8,9},{9,10},{10,1... | collective-permute-start | bytes 6152 | tf_op jit(solution)/shard_map/ppermute | solution.py:23
  60.0 1.4 %collective-permute-start.20 = (f32[1,512]{1,0:T(1,128)S(1)}, f32[1,512]{1,0:T(1,128)S(1)}, u32[]{:S(2)}, u32[]{:S(2)}) collective-permute-start(f32[1,512]{1,0:T(1,128)S(1)} %get-tuple-element.48), channel_id=1, source_target_pairs={{1,0},{2,1},{3,2},{0,3},{5,4},{6,5},{7,6},{4,7},{9,8},{10,9},{11,1... | collective-permute-start | bytes 6152 | tf_op jit(solution)/shard_map/ppermute | solution.py:25
  60.1 3.1 %collective-permute-start.21 = (f32[1,512]{1,0:T(1,128)S(1)}, f32[1,512]{1,0:T(1,128)S(1)}, u32[]{:S(2)}, u32[]{:S(2)}) collective-permute-start(f32[1,512]{1,0:T(1,128)S(1)} %get-tuple-element.49), channel_id=1, source_target_pairs={{0,1},{1,2},{2,3},{3,0},{4,5},{5,6},{6,7},{7,4},{8,9},{9,10},{10,1... | collective-permute-start | bytes 6152 | tf_op jit(solution)/shard_map/ppermute | solution.py:23
  63.3 1.4 %collective-permute-start.22 = (f32[1,512]{1,0:T(1,128)S(1)}, f32[1,512]{1,0:T(1,128)S(1)}, u32[]{:S(2)}, u32[]{:S(2)}) collective-permute-start(f32[1,512]{1,0:T(1,128)S(1)} %get-tuple-element.46), channel_id=1, source_target_pairs={{1,0},{2,1},{3,2},{0,3},{5,4},{6,5},{7,6},{4,7},{9,8},{10,9},{11,1... | collective-permute-start | bytes 6152 | tf_op jit(solution)/shard_map/ppermute | solution.py:25
  63.4 3.1 %collective-permute-start.23 = (f32[1,512]{1,0:T(1,128)S(1)}, f32[1,512]{1,0:T(1,128)S(1)}, u32[]{:S(2)}, u32[]{:S(2)}) collective-permute-start(f32[1,512]{1,0:T(1,128)S(1)} %get-tuple-element.47), channel_id=1, source_target_pairs={{0,1},{1,2},{2,3},{3,0},{4,5},{5,6},{6,7},{7,4},{8,9},{9,10},{10,1... | collective-permute-start | bytes 6152 | tf_op jit(solution)/shard_map/ppermute | solution.py:23
  78.6 11.1 %all-to-all-start.3 = ((f32[8,3,4,512]{3,2,1,0:T(4,128)}), f32[8,3,4,512]{3,2,1,0:T(4,128)S(1)}, u32[]{:S(2)}, u32[]{:S(2)}) async-start(f32[8,3,4,512]{3,2,1,0:T(4,128)} %concatenate.115.clone), calls=%async_computation.3 | async-start | bytes 393216 | tf_op jit(solution)/shard_map/all_to_all | solution.py:106
where the time goes:
time: 90.9 us; the launch traced here: 90.6 us
  waiting for transfers between devices  38 us (42%)
  blocking collectives  34.5 us (38%)
  starting transfers between devices  12 us (13%)
  other arithmetic  4.07 us (4%)
  local copies, waits for them, and re-layouts  1.53 us (2%)
    all_to_all x2, blocking collectives, body(): lax.all_to_all(carried[None], 'tm', split_axis=2, concat_axis=0, tiled=True)  24.3 us
    ppermute x12, waiting for transfers between devices, padded_2(): lax.ppermute(tail, axis, [(i, (i + 1) % count) for i in range(count)])  21.1 us
    all_to_all x1, blocking collectives, body(): lax.all_to_all(running, 'tm', split_axis=0, concat_axis=2, tiled=True)[0]  10.2 us
    ppermute x12, waiting for transfers between devices, padded_2(): lax.ppermute(head, axis, [((i + 1) % count, i) for i in range(count)])  9.29 us
    all_to_all x1, waiting for transfers between devices, body(): lax.all_to_all(running, 'tm', split_axis=0, concat_axis=2, tiled=True)[0]  7.62 us
    ppermute x12, starting transfers between devices, padded_2(): lax.ppermute(tail, axis, [(i, (i + 1) % count) for i in range(count)])  5.47 us
    all_to_all x1, starting transfers between devices, body(): lax.all_to_all(running, 'tm', split_axis=0, concat_axis=2, tiled=True)[0]  3.39 us
    ppermute x12, starting transfers between devices, padded_2(): lax.ppermute(head, axis, [((i + 1) % count, i) for i in range(count)])  3.12 us
  transfers between devices with their start and end apart: 25, of which 25 were waited for; matrix products, arithmetic and copies ran while one was open for 1% of the time, Pallas kernels for 0%

commit v1 on v0

--- a/solution.py
+++ b/solution.py
@@ -11,6 +11,13 @@
 DEPTH_MAX = 1.5
 GRAVITY = 1.0
 TURN_RATE = 0.15
+
+
+def swap_blocks(block, axis, split, join):
+    n_dev = lax.axis_size(axis)
+    blocks = jnp.stack(jnp.split(block, n_dev, axis=split), axis=0)
+    blocks = lax.all_to_all(blocks, axis, split_axis=0, concat_axis=0)
+    return jnp.concatenate(blocks, axis=join)
 
 
 def padded_2(cells, sides, width):
@@ -103,7 +110,7 @@
         stacked = lax.all_to_all(carried[None], "tm", split_axis=2, concat_axis=0, tiled=True)
         running = jnp.cumsum(stacked, axis=0)
         running = jnp.concatenate([jnp.zeros_like(stacked[:1]), running[:-1]], axis=0)
-        before = lax.all_to_all(running, "tm", split_axis=0, concat_axis=2, tiled=True)[0]
+        before = swap_blocks(running, "tm", 0, 2)[0]
         total = start + before
         if round_index + 1 < ROUNDS:
             guess = rotate(total, number * turning)

time: 90.9 us -> 96.4 us (1.061)
  blocking collectives: 34.5 us -> 10.2 us
  waiting for transfers between devices: 38 us -> 53 us
  starting transfers between devices: 12 us -> 21.2 us
  local copies, waits for them, and re-layouts: 1.53 us -> 7.04 us
    all_to_all x3 -> x1, blocking collectives: 34.5 us -> 10.2 us  [swap_blocks(): blocks = lax.all_to_all(blocks, axis, split_axis=0, concat_axis=0)]
    all_to_all x1 -> x3, waiting for transfers between devices: 7.62 us -> 22.6 us  [the longest x2 15 us: body(): lax.all_to_all(carried[None], 'tm', split_axis=2, concat_axis=0, tiled=True)]
    all_to_all x1 -> x3, starting transfers between devices: 3.39 us -> 12.6 us  [the longest x2 9.2 us: body(): lax.all_to_all(carried[None], 'tm', split_axis=2, concat_axis=0, tiled=True)]
    unnamed x6 -> x18, local copies, waits for them, and re-layouts: 0.04 us -> 4.35 us
    broadcast_in_dim x2, local copies, waits for them, and re-layouts: 0.41 us -> 1.76 us  [body(): carried[None]]
  transfers between devices with their start and end apart: 25 -> 27, of which waited for: 25 -> 27; matrix products, arithmetic and copies ran while one was open for 1% -> 2% of each run, Pallas kernels for 0% -> 0%
where the time goes in v1:
time: 96.4 us; the launch traced here: 96 us
  waiting for transfers between devices  53 us (55%)
  starting transfers between devices  21.2 us (22%)
  blocking collectives  10.2 us (11%)
  local copies, waits for them, and re-layouts  7.04 us (7%)
  other arithmetic  4.07 us (4%)
    ppermute x12, waiting for transfers between devices, padded_2(): lax.ppermute(tail, axis, [(i, (i + 1) % count) for i in range(count)])  21.1 us
    all_to_all x2, waiting for transfers between devices, body(): lax.all_to_all(carried[None], 'tm', split_axis=2, concat_axis=0, tiled=True)  15 us
    all_to_all x1, blocking collectives, swap_blocks(): blocks = lax.all_to_all(blocks, axis, split_axis=0, concat_axis=0)  10.2 us
    ppermute x12, waiting for transfers between devices, padded_2(): lax.ppermute(head, axis, [((i + 1) % count, i) for i in range(count)])  9.29 us
    all_to_all x2, starting transfers between devices, body(): lax.all_to_all(carried[None], 'tm', split_axis=2, concat_axis=0, tiled=True)  9.2 us
    all_to_all x1, waiting for transfers between devices, swap_blocks(): blocks = lax.all_to_all(blocks, axis, split_axis=0, concat_axis=0)  7.63 us
    ppermute x12, starting transfers between devices, padded_2(): lax.ppermute(tail, axis, [(i, (i + 1) % count) for i in range(count)])  5.47 us
    unnamed x18, local copies, waits for them, and re-layouts  4.35 us
  transfers between devices with their start and end apart: 27, of which 27 were waited for; matrix products, arithmetic and copies ran while one was open for 2% of the time, Pallas kernels for 0%

profile of v1, /device:TPU:0, one launch (start us, length us, event | category | flops | bytes accessed | tf_op | source)
XLA Modules:
  0.0 96.0 jit_solution(14518451957335326506)
XLA Ops:
  0.2 1.0 %multiply_multiply_fusion.5 = (f32[32,512]{1,0:T(8,128)S(1)}, f32[32,512]{1,0:T(8,128)S(1)}, f32[32,512]{1,0:T(8,128)S(1)}) fusion(f32[32,512]{1,0:T(8,128)} %param.3, f32[512]{0:T(512)S(1)} %fusion.117, f32[512]{0:T(512)S(1)} %get-tuple-element.70, f32[3,32,512]{2,1,0:T(8,128)} %param.2, f32[512]{0:T(512)S(1)} %get-tuple-element.71), kind=kLoop, calls=%fused_computation.196 | loop fusion | flops 147456 | bytes 399360 | tf_op jit(solution)/shard_map/mul | solution.py:66
  1.1 2.5 %collective-permute-start = (f32[1,512]{1,0:T(1,128)S(1)}, f32[1,512]{1,0:T(1,128)S(1)}, u32[]{:S(2)}, u32[]{:S(2)}) collective-permute-start(f32[1,512]{1,0:T(1,128)S(1)} %get-tuple-element.68), channel_id=1, source_target_pairs={{1,0},{2,1},{3,2},{0,3},{5,4},{6,5},{7,6},{4,7},{9,8},{10,9},{11,1... | collective-permute-start | bytes 6152 | tf_op jit(solution)/shard_map/ppermute | solution.py:32
  3.8 1.1 %collective-permute-done = f32[1,512]{1,0:T(1,128)S(1)} collective-permute-done((f32[1,512]{1,0:T(1,128)S(1)}, f32[1,512]{1,0:T(1,128)S(1)}, u32[]{:S(2)}, u32[]{:S(2)}) %collective-permute-start) | collective-permute-done | bytes 2080 | tf_op jit(solution)/shard_map/ppermute | solution.py:32
  4.9 1.7 %collective-permute-done.1 = f32[1,512]{1,0:T(1,128)S(1)} collective-permute-done((f32[1,512]{1,0:T(1,128)S(1)}, f32[1,512]{1,0:T(1,128)S(1)}, u32[]{:S(2)}, u32[]{:S(2)}) %collective-permute-start.1) | collective-permute-done | bytes 2080 | tf_op jit(solution)/shard_map/ppermute | solution.py:30
  6.6 0.1 fusion.11
  6.8 0.5 collective-permute-start.3
  7.4 0.8 collective-permute-done.2
  8.1 1.8 %collective-permute-done.3 = f32[1,512]{1,0:T(1,128)S(1)} collective-permute-done((f32[1,512]{1,0:T(1,128)S(1)}, f32[1,512]{1,0:T(1,128)S(1)}, u32[]{:S(2)}, u32[]{:S(2)}) %collective-permute-start.3) | collective-permute-done | bytes 2080 | tf_op jit(solution)/shard_map/ppermute | solution.py:30
  10.0 0.5 collective-permute-start.5
  10.5 0.1 multiply_multiply_fusion.4
  10.6 0.7 collective-permute-done.4
  11.3 1.8 %collective-permute-done.5 = f32[1,512]{1,0:T(1,128)S(1)} collective-permute-done((f32[1,512]{1,0:T(1,128)S(1)}, f32[1,512]{1,0:T(1,128)S(1)}, u32[]{:S(2)}, u32[]{:S(2)}) %collective-permute-start.5) | collective-permute-done | bytes 2080 | tf_op jit(solution)/shard_map/ppermute | solution.py:30
  13.3 0.5 collective-permute-start.7
  13.8 0.8 collective-permute-done.6
  14.6 1.8 %collective-permute-done.7 = f32[1,512]{1,0:T(1,128)S(1)} collective-permute-done((f32[1,512]{1,0:T(1,128)S(1)}, f32[1,512]{1,0:T(1,128)S(1)}, u32[]{:S(2)}, u32[]{:S(2)}) %collective-permute-start.7) | collective-permute-done | bytes 2080 | tf_op jit(solution)/shard_map/ppermute | solution.py:30
  16.5 0.5 collective-permute-start.9
  17.0 0.1 multiply_multiply_fusion.3
  17.1 0.7 collective-permute-done.8
  17.8 1.8 %collective-permute-done.9 = f32[1,512]{1,0:T(1,128)S(1)} collective-permute-done((f32[1,512]{1,0:T(1,128)S(1)}, f32[1,512]{1,0:T(1,128)S(1)}, u32[]{:S(2)}, u32[]{:S(2)}) %collective-permute-start.9) | collective-permute-done | bytes 2080 | tf_op jit(solution)/shard_map/ppermute | solution.py:30
  19.5 0.1 fusion.31
  19.7 0.5 collective-permute-start.11
  20.3 0.7 collective-permute-done.10
  21.0 1.8 %collective-permute-done.11 = f32[1,512]{1,0:T(1,128)S(1)} collective-permute-done((f32[1,512]{1,0:T(1,128)S(1)}, f32[1,512]{1,0:T(1,128)S(1)}, u32[]{:S(2)}, u32[]{:S(2)}) %collective-permute-start.11) | collective-permute-done | bytes 2080 | tf_op jit(solution)/shard_map/ppermute | solution.py:30
  22.8 0.1 fusion.133
  23.0 0.9 copy.80
  23.9 5.8 %all-to-all-start = ((f32[1,3,32,512]{3,0,1,2:T(1,128)}), f32[1,3,32,512]{3,0,1,2:T(1,128)S(1)}, u32[]{:S(2)}, u32[]{:S(2)}) async-start(f32[1,3,32,512]{3,0,1,2:T(1,128)} %copy.80), calls=%async_computation | async-start | bytes 393216 | tf_op jit(solution)/shard_map/all_to_all | solution.py:110
  29.7 7.8 %all-to-all-done = f32[1,3,32,512]{3,0,1,2:T(1,128)S(1)} async-done(((f32[1,3,32,512]{3,0,1,2:T(1,128)}), f32[1,3,32,512]{3,0,1,2:T(1,128)S(1)}, u32[]{:S(2)}, u32[]{:S(2)}) %all-to-all-start) | async-done | bytes 196640 | tf_op jit(solution)/shard_map/all_to_all | solution.py:110
  37.7 10.2 %all_to_all.46 = f32[8,1,3,4,512]{4,3,2,1,0:T(4,128)S(1)} all-to-all(f32[8,1,3,4,512]{4,3,2,1,0:T(4,128)S(1)} %constant_dynamic-update-slice_fusion), channel_id=1, replica_groups=mesh['tm'=8,'lon'=4] {'tm'}, dimensions={0} | all-to-all | bytes 393216 | tf_op jit(solution)/shard_map/all_to_all | solution.py:19
  48.1 0.5 collective-permute-start.13
  48.6 0.8 collective-permute-done.12
  49.4 1.8 %collective-permute-done.13 = f32[1,512]{1,0:T(1,128)S(1)} collective-permute-done((f32[1,512]{1,0:T(1,128)S(1)}, f32[1,512]{1,0:T(1,128)S(1)}, u32[]{:S(2)}, u32[]{:S(2)}) %collective-permute-start.13) | collective-permute-done | bytes 2080 | tf_op jit(solution)/shard_map/ppermute | solution.py:30
  51.4 0.5 collective-permute-start.15
  51.9 0.8 collective-permute-done.14
  52.7 1.8 %collective-permute-done.15 = f32[1,512]{1,0:T(1,128)S(1)} collective-permute-done((f32[1,512]{1,0:T(1,128)S(1)}, f32[1,512]{1,0:T(1,128)S(1)}, u32[]{:S(2)}, u32[]{:S(2)}) %collective-permute-start.15) | collective-permute-done | bytes 2080 | tf_op jit(solution)/shard_map/ppermute | solution.py:30
  54.6 0.5 collective-permute-start.17
  55.0 0.1 multiply_multiply_fusion.1
  55.2 0.7 collective-permute-done.16
  55.9 1.8 %collective-permute-done.17 = f32[1,512]{1,0:T(1,128)S(1)} collective-permute-done((f32[1,512]{1,0:T(1,128)S(1)}, f32[1,512]{1,0:T(1,128)S(1)}, u32[]{:S(2)}, u32[]{:S(2)}) %collective-permute-start.17) | collective-permute-done | bytes 2080 | tf_op jit(solution)/shard_map/ppermute | solution.py:30
  57.8 0.5 collective-permute-start.19
  58.3 0.8 collective-permute-done.18
  59.1 1.8 %collective-permute-done.19 = f32[1,512]{1,0:T(1,128)S(1)} collective-permute-done((f32[1,512]{1,0:T(1,128)S(1)}, f32[1,512]{1,0:T(1,128)S(1)}, u32[]{:S(2)}, u32[]{:S(2)}) %collective-permute-start.19) | collective-permute-done | bytes 2080 | tf_op jit(solution)/shard_map/ppermute | solution.py:30
  61.0 0.5 collective-permute-start.21
  61.5 0.1 multiply_multiply_fusion
  61.6 0.7 collective-permute-done.20
  62.3 1.8 %collective-permute-done.21 = f32[1,512]{1,0:T(1,128)S(1)} collective-permute-done((f32[1,512]{1,0:T(1,128)S(1)}, f32[1,512]{1,0:T(1,128)S(1)}, u32[]{:S(2)}, u32[]{:S(2)}) %collective-permute-start.21) | collective-permute-done | bytes 2080 | tf_op jit(solution)/shard_map/ppermute | solution.py:30
  64.0 0.1 fusion.62
  64.2 0.5 collective-permute-start.23
  64.8 0.8 collective-permute-done.22
  65.5 1.8 %collective-permute-done.23 = f32[1,512]{1,0:T(1,128)S(1)} collective-permute-done((f32[1,512]{1,0:T(1,128)S(1)}, f32[1,512]{1,0:T(1,128)S(1)}, u32[]{:S(2)}, u32[]{:S(2)}) %collective-permute-start.23) | collective-permute-done | bytes 2080 | tf_op jit(solution)/shard_map/ppermute | solution.py:30
  67.3 0.1 fusion.134
  67.5 0.9 copy.89
  68.4 3.4 %all-to-all-start.2 = ((f32[1,3,32,512]{3,0,1,2:T(1,128)}), f32[1,3,32,512]{3,0,1,2:T(1,128)S(1)}, u32[]{:S(2)}, u32[]{:S(2)}) async-start(f32[1,3,32,512]{3,0,1,2:T(1,128)} %copy.89), calls=%async_computation.2 | async-start | bytes 393216 | tf_op jit(solution)/shard_map/all_to_all | solution.py:110
  71.8 0.6 constant_dynamic-update-slice_fusion.15
  72.4 7.2 %all-to-all-done.2 = f32[1,3,32,512]{3,0,1,2:T(1,128)S(1)} async-done(((f32[1,3,32,512]{3,0,1,2:T(1,128)}), f32[1,3,32,512]{3,0,1,2:T(1,128)S(1)}, u32[]{:S(2)}, u32[]{:S(2)}) %all-to-all-start.2) | async-done | bytes 196640 | tf_op jit(solution)/shard_map/all_to_all | solution.py:110
  79.7 0.6 constant_dynamic-update-slice_fusion.14
  80.3 0.6 constant_dynamic-update-slice_fusion.13
  80.9 0.6 constant_dynamic-update-slice_fusion.12
  81.6 0.6 constant_dynamic-update-slice_fusion.11
  82.2 0.6 constant_dynamic-update-slice_fusion.10
  82.8 0.6 constant_dynamic-update-slice_fusion.9
  83.4 0.6 constant_dynamic-update-slice_fusion.8
  84.0 3.4 %all-to-all-start.3 = ((f32[8,1,3,4,512]{4,3,2,1,0:T(4,128)}), f32[8,1,3,4,512]{4,3,2,1,0:T(4,128)S(1)}, u32[]{:S(2)}, u32[]{:S(2)}) async-start(f32[8,1,3,4,512]{4,3,2,1,0:T(4,128)} %constant_dynamic-update-slice_fusion.8), calls=%async_computation.3 | async-start | bytes 393216 | tf_op jit(solution)/shard_map/all_to_all | solution.py:19
  87.5 7.6 %all-to-all-done.3 = f32[8,1,3,4,512]{4,3,2,1,0:T(4,128)S(1)} async-done(((f32[8,1,3,4,512]{4,3,2,1,0:T(4,128)}), f32[8,1,3,4,512]{4,3,2,1,0:T(4,128)S(1)}, u32[]{:S(2)}, u32[]{:S(2)}) %all-to-all-start.3) | async-done | bytes 196640 | tf_op jit(solution)/shard_map/all_to_all | solution.py:19
  95.3 0.7 maximum_bitcast_fusion.1
  (71 shorter events, 2.5 us)
Async XLA Ops:
  0.1 6.5 %copy-start.1 = (f32[3,32,512]{2,1,0:T(8,128)S(1)}, f32[3,32,512]{2,1,0:T(8,128)}, u32[]{:S(2)}) copy-start(f32[3,32,512]{2,1,0:T(8,128)} %param.2) | copy-start | bytes 589828
  1.1 3.8 %collective-permute-start = (f32[1,512]{1,0:T(1,128)S(1)}, f32[1,512]{1,0:T(1,128)S(1)}, u32[]{:S(2)}, u32[]{:S(2)}) collective-permute-start(f32[1,512]{1,0:T(1,128)S(1)} %get-tuple-element.68), channel_id=1, source_target_pairs={{1,0},{2,1},{3,2},{0,3},{5,4},{6,5},{7,6},{4,7},{9,8},{10,9},{11,1... | collective-permute-start | bytes 6152 | tf_op jit(solution)/shard_map/ppermute | solution.py:32
  3.6 3.0 %collective-permute-start.1 = (f32[1,512]{1,0:T(1,128)S(1)}, f32[1,512]{1,0:T(1,128)S(1)}, u32[]{:S(2)}, u32[]{:S(2)}) collective-permute-start(f32[1,512]{1,0:T(1,128)S(1)} %get-tuple-element.69), channel_id=1, source_target_pairs={{0,1},{1,2},{2,3},{3,0},{4,5},{5,6},{6,7},{7,4},{8,9},{9,10},{10,1... | collective-permute-start | bytes 6152 | tf_op jit(solution)/shard_map/ppermute | solution.py:30
  6.6 3.3 %copy-start = (f32[32,512]{1,0:T(8,128)S(1)}, f32[32,512]{1,0:T(8,128)}, u32[]{:S(2)}) copy-start(f32[32,512]{1,0:T(8,128)} %param.3) | copy-start | bytes 196612
  6.8 1.4 %collective-permute-start.2 = (f32[1,512]{1,0:T(1,128)S(1)}, f32[1,512]{1,0:T(1,128)S(1)}, u32[]{:S(2)}, u32[]{:S(2)}) collective-permute-start(f32[1,512]{1,0:T(1,128)S(1)} %get-tuple-element.66), channel_id=1, source_target_pairs={{1,0},{2,1},{3,2},{0,3},{5,4},{6,5},{7,6},{4,7},{9,8},{10,9},{11,1... | collective-permute-start | bytes 6152 | tf_op jit(solution)/shard_map/ppermute | solution.py:32
  6.8 3.1 %collective-permute-start.3 = (f32[1,512]{1,0:T(1,128)S(1)}, f32[1,512]{1,0:T(1,128)S(1)}, u32[]{:S(2)}, u32[]{:S(2)}) collective-permute-start(f32[1,512]{1,0:T(1,128)S(1)} %get-tuple-element.67), channel_id=1, source_target_pairs={{0,1},{1,2},{2,3},{3,0},{4,5},{5,6},{6,7},{7,4},{8,9},{9,10},{10,1... | collective-permute-start | bytes 6152 | tf_op jit(solution)/shard_map/ppermute | solution.py:30
  10.0 1.4 %collective-permute-start.4 = (f32[1,512]{1,0:T(1,128)S(1)}, f32[1,512]{1,0:T(1,128)S(1)}, u32[]{:S(2)}, u32[]{:S(2)}) collective-permute-start(f32[1,512]{1,0:T(1,128)S(1)} %get-tuple-element.64), channel_id=1, source_target_pairs={{1,0},{2,1},{3,2},{0,3},{5,4},{6,5},{7,6},{4,7},{9,8},{10,9},{11,1... | collective-permute-start | bytes 6152 | tf_op jit(solution)/shard_map/ppermute | solution.py:32
  10.0 3.1 %collective-permute-start.5 = (f32[1,512]{1,0:T(1,128)S(1)}, f32[1,512]{1,0:T(1,128)S(1)}, u32[]{:S(2)}, u32[]{:S(2)}) collective-permute-start(f32[1,512]{1,0:T(1,128)S(1)} %get-tuple-element.65), channel_id=1, source_target_pairs={{0,1},{1,2},{2,3},{3,0},{4,5},{5,6},{6,7},{7,4},{8,9},{9,10},{10,1... | collective-permute-start | bytes 6152 | tf_op jit(solution)/shard_map/ppermute | solution.py:30
  13.2 1.4 %collective-permute-start.6 = (f32[1,512]{1,0:T(1,128)S(1)}, f32[1,512]{1,0:T(1,128)S(1)}, u32[]{:S(2)}, u32[]{:S(2)}) collective-permute-start(f32[1,512]{1,0:T(1,128)S(1)} %get-tuple-element.62), channel_id=1, source_target_pairs={{1,0},{2,1},{3,2},{0,3},{5,4},{6,5},{7,6},{4,7},{9,8},{10,9},{11,1... | collective-permute-start | bytes 6152 | tf_op jit(solution)/shard_map/ppermute | solution.py:32
  13.3 3.1 %collective-permute-start.7 = (f32[1,512]{1,0:T(1,128)S(1)}, f32[1,512]{1,0:T(1,128)S(1)}, u32[]{:S(2)}, u32[]{:S(2)}) collective-permute-start(f32[1,512]{1,0:T(1,128)S(1)} %get-tuple-element.63), channel_id=1, source_target_pairs={{0,1},{1,2},{2,3},{3,0},{4,5},{5,6},{6,7},{7,4},{8,9},{9,10},{10,1... | collective-permute-start | bytes 6152 | tf_op jit(solution)/shard_map/ppermute | solution.py:30
  16.4 1.4 %collective-permute-start.8 = (f32[1,512]{1,0:T(1,128)S(1)}, f32[1,512]{1,0:T(1,128)S(1)}, u32[]{:S(2)}, u32[]{:S(2)}) collective-permute-start(f32[1,512]{1,0:T(1,128)S(1)} %get-tuple-element.60), channel_id=1, source_target_pairs={{1,0},{2,1},{3,2},{0,3},{5,4},{6,5},{7,6},{4,7},{9,8},{10,9},{11,1... | collective-permute-start | bytes 6152 | tf_op jit(solution)/shard_map/ppermute | solution.py:32
  16.5 3.1 %collective-permute-start.9 = (f32[1,512]{1,0:T(1,128)S(1)}, f32[1,512]{1,0:T(1,128)S(1)}, u32[]{:S(2)}, u32[]{:S(2)}) collective-permute-start(f32[1,512]{1,0:T(1,128)S(1)} %get-tuple-element.61), channel_id=1, source_target_pairs={{0,1},{1,2},{2,3},{3,0},{4,5},{5,6},{6,7},{7,4},{8,9},{9,10},{10,1... | collective-permute-start | bytes 6152 | tf_op jit(solution)/shard_map/ppermute | solution.py:30
  19.7 1.4 %collective-permute-start.10 = (f32[1,512]{1,0:T(1,128)S(1)}, f32[1,512]{1,0:T(1,128)S(1)}, u32[]{:S(2)}, u32[]{:S(2)}) collective-permute-start(f32[1,512]{1,0:T(1,128)S(1)} %get-tuple-element.58), channel_id=1, source_target_pairs={{1,0},{2,1},{3,2},{0,3},{5,4},{6,5},{7,6},{4,7},{9,8},{10,9},{11,1... | collective-permute-start | bytes 6152 | tf_op jit(solution)/shard_map/ppermute | solution.py:32
  19.7 3.1 %collective-permute-start.11 = (f32[1,512]{1,0:T(1,128)S(1)}, f32[1,512]{1,0:T(1,128)S(1)}, u32[]{:S(2)}, u32[]{:S(2)}) collective-permute-start(f32[1,512]{1,0:T(1,128)S(1)} %get-tuple-element.59), channel_id=1, source_target_pairs={{0,1},{1,2},{2,3},{3,0},{4,5},{5,6},{6,7},{7,4},{8,9},{9,10},{10,1... | collective-permute-start | bytes 6152 | tf_op jit(solution)/shard_map/ppermute | solution.py:30
  23.9 13.6 %all-to-all-start = ((f32[1,3,32,512]{3,0,1,2:T(1,128)}), f32[1,3,32,512]{3,0,1,2:T(1,128)S(1)}, u32[]{:S(2)}, u32[]{:S(2)}) async-start(f32[1,3,32,512]{3,0,1,2:T(1,128)} %copy.80), calls=%async_computation | async-start | bytes 393216 | tf_op jit(solution)/shard_map/all_to_all | solution.py:110
  48.0 1.4 %collective-permute-start.12 = (f32[1,512]{1,0:T(1,128)S(1)}, f32[1,512]{1,0:T(1,128)S(1)}, u32[]{:S(2)}, u32[]{:S(2)}) collective-permute-start(f32[1,512]{1,0:T(1,128)S(1)} %get-tuple-element.56), channel_id=1, source_target_pairs={{1,0},{2,1},{3,2},{0,3},{5,4},{6,5},{7,6},{4,7},{9,8},{10,9},{11,1... | collective-permute-start | bytes 6152 | tf_op jit(solution)/shard_map/ppermute | solution.py:32
  48.1 3.1 %collective-permute-start.13 = (f32[1,512]{1,0:T(1,128)S(1)}, f32[1,512]{1,0:T(1,128)S(1)}, u32[]{:S(2)}, u32[]{:S(2)}) collective-permute-start(f32[1,512]{1,0:T(1,128)S(1)} %get-tuple-element.57), channel_id=1, source_target_pairs={{0,1},{1,2},{2,3},{3,0},{4,5},{5,6},{6,7},{7,4},{8,9},{9,10},{10,1... | collective-permute-start | bytes 6152 | tf_op jit(solution)/shard_map/ppermute | solution.py:30
  51.3 1.4 %collective-permute-start.14 = (f32[1,512]{1,0:T(1,128)S(1)}, f32[1,512]{1,0:T(1,128)S(1)}, u32[]{:S(2)}, u32[]{:S(2)}) collective-permute-start(f32[1,512]{1,0:T(1,128)S(1)} %get-tuple-element.54), channel_id=1, source_target_pairs={{1,0},{2,1},{3,2},{0,3},{5,4},{6,5},{7,6},{4,7},{9,8},{10,9},{11,1... | collective-permute-start | bytes 6152 | tf_op jit(solution)/shard_map/ppermute | solution.py:32
  51.4 3.1 %collective-permute-start.15 = (f32[1,512]{1,0:T(1,128)S(1)}, f32[1,512]{1,0:T(1,128)S(1)}, u32[]{:S(2)}, u32[]{:S(2)}) collective-permute-start(f32[1,512]{1,0:T(1,128)S(1)} %get-tuple-element.55), channel_id=1, source_target_pairs={{0,1},{1,2},{2,3},{3,0},{4,5},{5,6},{6,7},{7,4},{8,9},{9,10},{10,1... | collective-permute-start | bytes 6152 | tf_op jit(solution)/shard_map/ppermute | solution.py:30
  54.5 1.4 %collective-permute-start.16 = (f32[1,512]{1,0:T(1,128)S(1)}, f32[1,512]{1,0:T(1,128)S(1)}, u32[]{:S(2)}, u32[]{:S(2)}) collective-permute-start(f32[1,512]{1,0:T(1,128)S(1)} %get-tuple-element.52), channel_id=1, source_target_pairs={{1,0},{2,1},{3,2},{0,3},{5,4},{6,5},{7,6},{4,7},{9,8},{10,9},{11,1... | collective-permute-start | bytes 6152 | tf_op jit(solution)/shard_map/ppermute | solution.py:32
  54.6 3.1 %collective-permute-start.17 = (f32[1,512]{1,0:T(1,128)S(1)}, f32[1,512]{1,0:T(1,128)S(1)}, u32[]{:S(2)}, u32[]{:S(2)}) collective-permute-start(f32[1,512]{1,0:T(1,128)S(1)} %get-tuple-element.53), channel_id=1, source_target_pairs={{0,1},{1,2},{2,3},{3,0},{4,5},{5,6},{6,7},{7,4},{8,9},{9,10},{10,1... | collective-permute-start | bytes 6152 | tf_op jit(solution)/shard_map/ppermute | solution.py:30
  57.7 1.4 %collective-permute-start.18 = (f32[1,512]{1,0:T(1,128)S(1)}, f32[1,512]{1,0:T(1,128)S(1)}, u32[]{:S(2)}, u32[]{:S(2)}) collective-permute-start(f32[1,512]{1,0:T(1,128)S(1)} %get-tuple-element.50), channel_id=1, source_target_pairs={{1,0},{2,1},{3,2},{0,3},{5,4},{6,5},{7,6},{4,7},{9,8},{10,9},{11,1... | collective-permute-start | bytes 6152 | tf_op jit(solution)/shard_map/ppermute | solution.py:32
  57.8 3.1 %collective-permute-start.19 = (f32[1,512]{1,0:T(1,128)S(1)}, f32[1,512]{1,0:T(1,128)S(1)}, u32[]{:S(2)}, u32[]{:S(2)}) collective-permute-start(f32[1,512]{1,0:T(1,128)S(1)} %get-tuple-element.51), channel_id=1, source_target_pairs={{0,1},{1,2},{2,3},{3,0},{4,5},{5,6},{6,7},{7,4},{8,9},{9,10},{10,1... | collective-permute-start | bytes 6152 | tf_op jit(solution)/shard_map/ppermute | solution.py:30
  60.9 1.4 %collective-permute-start.20 = (f32[1,512]{1,0:T(1,128)S(1)}, f32[1,512]{1,0:T(1,128)S(1)}, u32[]{:S(2)}, u32[]{:S(2)}) collective-permute-start(f32[1,512]{1,0:T(1,128)S(1)} %get-tuple-element.48), channel_id=1, source_target_pairs={{1,0},{2,1},{3,2},{0,3},{5,4},{6,5},{7,6},{4,7},{9,8},{10,9},{11,1... | collective-permute-start | bytes 6152 | tf_op jit(solution)/shard_map/ppermute | solution.py:32
  61.0 3.1 %collective-permute-start.21 = (f32[1,512]{1,0:T(1,128)S(1)}, f32[1,512]{1,0:T(1,128)S(1)}, u32[]{:S(2)}, u32[]{:S(2)}) collective-permute-start(f32[1,512]{1,0:T(1,128)S(1)} %get-tuple-element.49), channel_id=1, source_target_pairs={{0,1},{1,2},{2,3},{3,0},{4,5},{5,6},{6,7},{7,4},{8,9},{9,10},{10,1... | collective-permute-start | bytes 6152 | tf_op jit(solution)/shard_map/ppermute | solution.py:30
  64.2 1.4 %collective-permute-start.22 = (f32[1,512]{1,0:T(1,128)S(1)}, f32[1,512]{1,0:T(1,128)S(1)}, u32[]{:S(2)}, u32[]{:S(2)}) collective-permute-start(f32[1,512]{1,0:T(1,128)S(1)} %get-tuple-element.46), channel_id=1, source_target_pairs={{1,0},{2,1},{3,2},{0,3},{5,4},{6,5},{7,6},{4,7},{9,8},{10,9},{11,1... | collective-permute-start | bytes 6152 | tf_op jit(solution)/shard_map/ppermute | solution.py:32
  64.2 3.1 %collective-permute-start.23 = (f32[1,512]{1,0:T(1,128)S(1)}, f32[1,512]{1,0:T(1,128)S(1)}, u32[]{:S(2)}, u32[]{:S(2)}) collective-permute-start(f32[1,512]{1,0:T(1,128)S(1)} %get-tuple-element.47), channel_id=1, source_target_pairs={{0,1},{1,2},{2,3},{3,0},{4,5},{5,6},{6,7},{7,4},{8,9},{9,10},{10,1... | collective-permute-start | bytes 6152 | tf_op jit(solution)/shard_map/ppermute | solution.py:30
  68.4 11.2 %all-to-all-start.2 = ((f32[1,3,32,512]{3,0,1,2:T(1,128)}), f32[1,3,32,512]{3,0,1,2:T(1,128)S(1)}, u32[]{:S(2)}, u32[]{:S(2)}) async-start(f32[1,3,32,512]{3,0,1,2:T(1,128)} %copy.89), calls=%async_computation.2 | async-start | bytes 393216 | tf_op jit(solution)/shard_map/all_to_all | solution.py:110
  84.0 11.1 %all-to-all-start.3 = ((f32[8,1,3,4,512]{4,3,2,1,0:T(4,128)}), f32[8,1,3,4,512]{4,3,2,1,0:T(4,128)S(1)}, u32[]{:S(2)}, u32[]{:S(2)}) async-start(f32[8,1,3,4,512]{4,3,2,1,0:T(4,128)} %constant_dynamic-update-slice_fusion.8), calls=%async_computation.3 | async-start | bytes 393216 | tf_op jit(solution)/shard_map/all_to_all | solution.py:19
